TPU v7x, 128 devices: a whole 4x4x4 slice. The times are simulated.
128 devices in a mesh: kt: 8 (over x_hi, z), ks: 16 (over y, x_lo, core).
Axes of the slice: x: 4 (x_hi: 2, x_lo: 2; x = x_hi * 2 + x_lo), y: 4, z: 4, core: 2. Of those that a mesh axis runs over, the one named last changes fastest.
Arguments:
- val_target: bfloat16 [16, 32, 512], P('kt', None, 'ks'), may hold values from -6 to 6
- cond_target: bfloat16 [16, 64, 512], P('kt', None, 'ks'), may hold values from -0.03125 to 0.03125
- val_source: bfloat16 [64, 32, 512], P('ks', None, 'kt'), may hold values from -6 to 6
- cond_source: bfloat16 [64, 64, 512], P('ks', None, 'kt'), may hold values from -0.125 to 0.125
- trial_vectors: bfloat16 [64, 16, 2048], P('ks', 'kt'), may hold values from -6 to 6
- screened: bfloat16 [512, 512, 512], P(None, ('kt', 'ks')), may hold values from -0.25 to 0.25
- pair_momentum: int32 [16, 64], replicated, may hold values from 0 to 511
Outputs:
- kernel_out: float32 [16, 16, 2048], P('kt', 'ks')
All inputs are finite; a program needn't handle non-finite values.
Results may differ from a plain program's by a relative error of at most 0.019.
Values may be sent and summed in bfloat16 or wider, within the bound.
No kernel may reach another device: no remote copies, remote signals or barrier semaphores. Data moves between devices by JAX's collectives and lax.ppermute only.
A program may use at most 128 MiB of HBM per device.

v0:
```python
import jax
import jax.numpy as jnp
from jax import lax
from jax.sharding import PartitionSpec as P


def rows_first(arrays, axis, dims):
    turned = [jnp.moveaxis(a, dim, 0) for a, dim in zip(arrays, dims)]
    both = jnp.concatenate([t.reshape(len(t), -1) for t in turned], axis=1)
    whole, at, finished = (lax.all_gather(both, axis, axis=0, tiled=True), 0, [])
    for t, dim in zip(turned, dims):
        slab = whole[:, at : at + t[0].size].reshape(-1, *t.shape[1:])
        finished.append(jnp.moveaxis(slab, 0, dim))
        at += t[0].size
    return tuple(finished)


def sent_together(arrays, axis, dim, along):
    ends, at = ([], 0)
    for a in arrays[:-1]:
        at += a.shape[along]
        ends.append(at)
    both = jnp.concatenate(arrays, axis=along)
    return tuple(jnp.split(lax.all_gather(both, axis, axis=dim, tiled=True), ends, axis=along))


def cut_along(x, dim, peers):
    before, after = (x.shape[:dim], x.shape[dim + 1 :])
    return jnp.moveaxis(x.reshape(*before, peers, -1, *after), dim, 0)


def sum_at_owner(x, axis, dim):
    blocks = cut_along(x, dim, lax.axis_size(axis))
    arrived = lax.all_to_all(blocks, axis, split_axis=0, concat_axis=0, tiled=True)
    return arrived.astype(jnp.float32).sum(axis=0)


def local(val_target, cond_target, val_source, cond_source, trial_vectors, screened, pair_momentum):
    tgt_val, tgt_cond = rows_first((val_target, cond_target), "ks", (2, 2))
    src_val, src_cond, vectors = (
        *sent_together((val_source, cond_source), "kt", 2, 1),
        lax.all_gather(trial_vectors, "kt", axis=1, tiled=True),
    )
    count_kt = lax.axis_size("kt")
    count_ks = lax.axis_size("ks")
    tgt_count = tgt_val.shape[0]
    src_count = src_val.shape[0]
    pair_count = tgt_count * src_count
    width = screened.shape[2]
    val_bands = tgt_val.shape[1]
    cond_bands = tgt_cond.shape[1]
    vec_count = vectors.shape[1]
    table = pair_momentum.reshape(count_kt, tgt_count, count_ks, src_count)
    table = table.transpose(1, 3, 0, 2).reshape(pair_count, count_kt * count_ks)
    outgoing = screened[table]
    arrived = lax.all_to_all(outgoing, ("kt", "ks"), split_axis=1, concat_axis=1, tiled=True)
    pair_mats = arrived.reshape(tgt_count, src_count, width, width)
    trial_four = vectors.reshape(src_count, vec_count, val_bands, cond_bands)
    dressed = jnp.einsum(
        "snwc,scq->snwq", trial_four, src_cond, preferred_element_type=jnp.float32
    ).astype(jnp.bfloat16)
    pair_prod = (
        tgt_val.astype(jnp.float32)[:, None, :, None, :]
        * src_val.astype(jnp.float32)[None, :, None, :, :]
    ).astype(jnp.bfloat16)
    kernels = jnp.einsum(
        "tsvwp,tspq->tsvwq", pair_prod, pair_mats, preferred_element_type=jnp.float32
    ).astype(jnp.bfloat16)
    reduced = jnp.einsum(
        "tsvwq,snwq->tvnq", kernels, dressed, preferred_element_type=jnp.float32
    ).astype(jnp.bfloat16)
    partial_out = jnp.einsum(
        "tvnq,tcq->tnvc", reduced, tgt_cond, preferred_element_type=jnp.float32
    )
    partial_out = partial_out.reshape(tgt_count, vec_count, val_bands * cond_bands)
    return sum_at_owner(partial_out.astype(jnp.bfloat16), "ks", 1)


def solution(mesh):
    in_specs = (
        P("kt", None, "ks"),
        P("kt", None, "ks"),
        P("ks", None, "kt"),
        P("ks", None, "kt"),
        P("ks", "kt", None),
        P(None, ("kt", "ks"), None),
        P(),
    )
    out_specs = P("kt", "ks", None)
    return jax.shard_map(local, mesh=mesh, in_specs=in_specs, out_specs=out_specs, check_vma=False)
```

profile of v0, /device:TPU:1, one launch (start us, length us, event | category | flops | bytes accessed | tf_op | source)
XLA Modules:
  0.0 284.5 jit_solution(2779591411790372973)
XLA Ops:
  0.0 0.9 reshape.72
  1.0 0.2 copy.98
  1.2 0.4 copy-done
  1.6 10.8 %gather_fusion = bf16[1024,4,512]{2,1,0:T(4,128)(2,1)} fusion(bf16[512,4,512]{2,1,0:T(4,128)(2,1)S(1)} %copy-done, s32[1024]{0:T(1024)S(1)} %fusion.16), kind=kCustom, calls=%fused_computation | custom fusion | bytes 8392704 | tf_op jit(solution)/shard_map/gather | solution.py:55
  12.4 6.5 %copy.100 = bf16[8,128,4,512]{3,2,0,1:T(4,128)(2,1)} copy(bf16[8,128,4,512]{3,2,1,0:T(4,128)(2,1)} %bitcast.54) | data formatting | bytes 8388608 | tf_op jit(solution)/shard_map/gather | solution.py:55
  18.9 12.0 %all-to-all-start = ((bf16[8,128,4,512]{3,2,0,1:T(4,128)(2,1)}), bf16[8,128,4,512]{3,2,0,1:T(4,128)(2,1)}, u32[]{:S(2)}, u32[]{:S(2)}) async-start(bf16[8,128,4,512]{3,2,0,1:T(4,128)(2,1)} %copy.100), calls=%async_computation | async-start | bytes 8388608 | tf_op jit(solution)/shard_map/all_to_all | solution.py:56
  31.2 59.9 %all_gather.9 = bf16[512,192]{1,0:T(8,128)(2,1)S(1)} all-gather(bf16[32,192]{1,0:T(8,128)(2,1)S(1)} %pad_maximum_fusion.1), channel_id=1, replica_groups=mesh['kt'=8,'ks'=16] {'ks'}, dimensions={0}, use_global_device_ids=true | all-gather | bytes 208896 | tf_op jit(solution)/shard_map/all_gather | solution.py:10
  91.6 30.6 %all_gather.10 = bf16[4,96,512]{1,0,2:T(4,128)(2,1)S(1)} all-gather(bf16[4,96,64]{1,0,2:T(4,128)(2,1)S(1)} %pad_maximum_fusion), channel_id=1, replica_groups=mesh['kt'=8,'ks'=16] {'kt'}, dimensions={2}, use_global_device_ids=true | all-gather | bytes 442368 | tf_op jit(solution)/shard_map/all_gather | solution.py:24
  122.2 0.4 split.8
  122.6 0.3 copy.118
  123.0 0.3 copy.116
  123.3 28.7 %all_gather.11 = bf16[4,16,2048]{2,0,1:T(4,128)(2,1)S(1)} all-gather(bf16[4,2,2048]{2,0,1:T(4,128)(2,1)S(1)} %copy.94), channel_id=1, replica_groups=mesh['kt'=8,'ks'=16] {'kt'}, dimensions={1}, use_global_device_ids=true | all-gather | bytes 294912 | tf_op jit(solution)/shard_map/all_gather | solution.py:42
  152.2 0.5 reshape.71
  152.7 0.7 convert_bitcast_fusion
  153.4 12.2 %copy.108 = bf16[4,16,32,512,1]{2,1,0,4,3:T(8,128)(2,1)} copy(bf16[4,16,32,512,1]{3,2,1,0,4:T(8,128)(2,1)S(1)} %convert_bitcast_fusion) | data formatting | bytes 4194304 | tf_op jit(solution)/shard_map/convert_element_type | solution.py:61
  165.7 5.6 %copy.101 = bf16[8,128,4,512]{3,2,1,0:T(4,128)(2,1)} copy(bf16[8,128,4,512]{3,2,0,1:T(4,128)(2,1)} %all-to-all-done) | data formatting | bytes 8388608 | tf_op jit(solution)/shard_map/all_to_all | solution.py:56
  171.3 6.9 %reshape.86 = bf16[2,4,512,512,1]{3,2,1,0,4:T(8,128)(2,1)} reshape(bf16[8,128,4,512]{3,2,1,0:T(4,128)(2,1)} %copy.101) | data formatting | bytes 8388608 | tf_op jit(solution)/shard_map/reshape | solution.py:57
  178.2 8.9 %fusion.3 = bf16[2,4,32,32,512]{4,3,2,1,0:T(8,128)(2,1)} fusion(f32[4,32,512]{2,1,0:T(8,128)S(1)} %convert_element_type.54, f32[2,32,512]{2,1,0:T(8,128)S(1)} %convert_bitcast_fusion.1, bf16[2,4,512,512,1]{3,2,1,0,4:T(8,128)(2,1)} %reshape.86), kind=kOutput, calls=%fused_computation.6 | convolution fusion | flops 4307550208 | bytes 12976128 | tf_op jit(solution)/shard_map/tsvwp,tspq->tsvwq/dot_general | solution.py:66
  187.1 44.3 %copy.103 = bf16[2,4,32,32,512]{3,2,1,0,4:T(8,128)(2,1)} copy(bf16[2,4,32,32,512]{4,3,2,1,0:T(8,128)(2,1)} %fusion.3) | data formatting | bytes 16777216 | tf_op jit(solution)/shard_map/convert_element_type | solution.py:68
  231.4 28.3 %fusion.4 = bf16[2,32,16,512]{1,2,0,3:T(8,128)(2,1)} fusion(bf16[4,16,32,512,1]{2,1,0,4,3:T(8,128)(2,1)} %copy.108, bf16[2,4,32,32,512]{3,2,1,0,4:T(8,128)(2,1)} %copy.103), kind=kOutput, calls=%fused_computation.7 | convolution fusion | flops 134742016 | bytes 11534336 | tf_op jit(solution)/shard_map/tsvwq,snwq->tvnq/dot_general | solution.py:69
  259.8 3.7 %fusion.11 = bf16[2,16,32,64]{3,2,1,0:T(8,128)(2,1)S(1)} fusion(bf16[2,64,512,1]{2,1,3,0:T(8,128)(2,1)S(1)} %bitcast.56, bf16[2,32,16,512]{1,2,0,3:T(8,128)(2,1)} %fusion.4), kind=kOutput, calls=%fused_computation.13 | convolution fusion | flops 67174400 | bytes 1310720 | tf_op jit(solution)/shard_map/tvnq,tcq->tnvc/dot_general | solution.py:72
  263.5 0.3 convert_element_type.61
  263.9 19.9 %all_to_all.10 = bf16[16,2,1,2048]{3,1,2,0:T(2,128)(2,1)S(1)} all-to-all(bf16[16,2,1,2048]{3,1,2,0:T(2,128)(2,1)S(1)} %bitcast.58), channel_id=1, replica_groups=mesh['kt'=8,'ks'=16] {'ks'}, dimensions={0} | all-to-all | bytes 262144 | tf_op jit(solution)/shard_map/all_to_all | solution.py:34
  283.9 0.6 reduce_sum.12
  (33 shorter events, 1.5 us)
Async XLA Ops:
  0.0 1.6 copy-start
  18.9 12.0 %copy-start.6 = (bf16[2,64,32]{1,2,0:T(8,128)(2,1)S(1)}, bf16[2,64,32]{1,2,0:T(8,128)(2,1)}, u32[]{:S(2)}) copy-start(bf16[2,64,32]{1,2,0:T(8,128)(2,1)} %param.8) | copy-start | bytes 24580
  18.9 12.1 %copy-start.5 = (bf16[2,32,32]{2,1,0:T(8,128)(2,1)S(1)}, bf16[2,32,32]{2,1,0:T(8,128)(2,1)}, u32[]{:S(2)}) copy-start(bf16[2,32,32]{2,1,0:T(8,128)(2,1)} %param.7) | copy-start | bytes 12292
  18.9 72.3 %copy-start.3 = (bf16[4,32,64]{2,1,0:T(8,128)(2,1)S(1)}, bf16[4,32,64]{2,1,0:T(8,128)(2,1)}, u32[]{:S(2)}) copy-start(bf16[4,32,64]{2,1,0:T(8,128)(2,1)} %param.9) | copy-start | bytes 49156
  18.9 72.5 %copy-start.2 = (bf16[4,64,64]{2,1,0:T(8,128)(2,1)S(1)}, bf16[4,64,64]{2,1,0:T(8,128)(2,1)}, u32[]{:S(2)}) copy-start(bf16[4,64,64]{2,1,0:T(8,128)(2,1)} %param.10) | copy-start | bytes 98308
  18.9 146.8 %all-to-all-start = ((bf16[8,128,4,512]{3,2,0,1:T(4,128)(2,1)}), bf16[8,128,4,512]{3,2,0,1:T(4,128)(2,1)}, u32[]{:S(2)}, u32[]{:S(2)}) async-start(bf16[8,128,4,512]{3,2,0,1:T(4,128)(2,1)} %copy.100), calls=%async_computation | async-start | bytes 8388608 | tf_op jit(solution)/shard_map/all_to_all | solution.py:56
  30.9 92.4 %copy-start.4 = (bf16[4,2,2048]{2,1,0:T(2,128)(2,1)S(1)}, bf16[4,2,2048]{2,1,0:T(2,128)(2,1)}, u32[]{:S(2)}) copy-start(bf16[4,2,2048]{2,1,0:T(2,128)(2,1)} %param.11) | copy-start | bytes 98308
  231.4 53.1 %copy-start.1 = (bf16[512,4,512]{2,1,0:T(4,128)(2,1)S(1)}, bf16[512,4,512]{2,1,0:T(4,128)(2,1)}, u32[]{:S(2)}) copy-start(bf16[512,4,512]{2,1,0:T(4,128)(2,1)} %param.12) | copy-start | bytes 6291460
where the time goes:
time: 285 us; the launch traced here: 284 us
  blocking collectives  139 us (49%)
  local copies, waits for them, and re-layouts  91.2 us (32%)
  matrix products  41.6 us (15%)
  starting transfers between devices  12 us (4%)
    all_gather x1, blocking collectives, rows_first(): lax.all_gather(both, axis, axis=0, tiled=True)  59.9 us
    convert_element_type x1, local copies, waits for them, and re-layouts, local(): kernels = jnp.einsum('tsvwp,tspq->tsvwq', pair_prod, pair_mats, preferred...  44.3 us
    all_gather x1, blocking collectives, sent_together(): lax.all_gather(both, axis, axis=dim, tiled=True)  30.6 us
    all_gather x1, blocking collectives, local(): lax.all_gather(trial_vectors, 'kt', axis=1, tiled=True)  28.7 us
    dot_general x1, matrix products, local(): jnp.einsum('tsvwq,snwq->tvnq', kernels, dressed, preferred_element_type=j...  28.3 us
    all_to_all x1, blocking collectives, sum_at_owner(): lax.all_to_all(blocks, axis, split_axis=0, concat_axis=0, tiled=True)  19.9 us
    gather x2, local copies, waits for them, and re-layouts, local(): outgoing = screened[table]  17.3 us
    convert_element_type x1, local copies, waits for them, and re-layouts, local(): dressed = jnp.einsum('snwc,scq->snwq', trial_four, src_cond, preferred_el...  12.2 us
  transfers between devices with their start and end apart: 1, of which 0 were waited for; matrix products, arithmetic and copies ran while one was open for 5% of the time, Pallas kernels for 0%

commit v1 on v0

--- a/solution.py
+++ b/solution.py
@@ -39,7 +39,9 @@
     tgt_val, tgt_cond = rows_first((val_target, cond_target), "ks", (2, 2))
     src_val, src_cond, vectors = (
         *sent_together((val_source, cond_source), "kt", 2, 1),
-        lax.all_gather(trial_vectors, "kt", axis=1, tiled=True),
+        jnp.concatenate(
+            lax.all_to_all(jnp.stack([trial_vectors] * lax.axis_size("kt")), "kt", 0, 0), axis=1
+        ),
     )
     count_kt = lax.axis_size("kt")
     count_ks = lax.axis_size("ks")

time: 285 us -> 259 us (0.909)
  blocking collectives: 139 us -> 105 us
  starting transfers between devices: 12 us -> 19.2 us
    all_gather x1 -> x0, blocking collectives: 28.7 us -> none  [local(): lax.all_gather(trial_vectors, 'kt', axis=1, tiled=True)]
    all_to_all x0 -> x1, starting transfers between devices: none -> 8.32 us  [local(): lax.all_to_all(jnp.stack([trial_vectors] * lax.axis_size('kt')), 'kt', 0, 0)]
    all_to_all x1, blocking collectives: 19.9 us -> 14.2 us  [sum_at_owner(): lax.all_to_all(blocks, axis, split_axis=0, concat_axis=0, tiled=True)]
  transfers between devices with their start and end apart: 1 -> 2, of which waited for: 0 -> 0; matrix products, arithmetic and copies ran while one was open for 5% -> 13% of each run, Pallas kernels for 0% -> 0%
where the time goes in v1:
time: 259 us; the launch traced here: 258 us
  blocking collectives  105 us (41%)
  local copies, waits for them, and re-layouts  92.4 us (36%)
  matrix products  41.6 us (16%)
  starting transfers between devices  19.2 us (7%)
    all_gather x1, blocking collectives, rows_first(): lax.all_gather(both, axis, axis=0, tiled=True)  60 us
    convert_element_type x1, local copies, waits for them, and re-layouts, local(): kernels = jnp.einsum('tsvwp,tspq->tsvwq', pair_prod, pair_mats, preferred...  44.3 us
    all_gather x1, blocking collectives, sent_together(): lax.all_gather(both, axis, axis=dim, tiled=True)  30.6 us
    dot_general x1, matrix products, local(): jnp.einsum('tsvwq,snwq->tvnq', kernels, dressed, preferred_element_type=j...  28.3 us
    gather x2, local copies, waits for them, and re-layouts, local(): outgoing = screened[table]  17.3 us
    all_to_all x1, blocking collectives, sum_at_owner(): lax.all_to_all(blocks, axis, split_axis=0, concat_axis=0, tiled=True)  14.2 us
    convert_element_type x1, local copies, waits for them, and re-layouts, local(): dressed = jnp.einsum('snwc,scq->snwq', trial_four, src_cond, preferred_el...  12.2 us
    all_to_all x1, starting transfers between devices, local(): lax.all_to_all(outgoing, ('kt', 'ks'), split_axis=1, concat_axis=1, tiled...  10.8 us
  transfers between devices with their start and end apart: 2, of which 0 were waited for; matrix products, arithmetic and copies ran while one was open for 13% of the time, Pallas kernels for 0%

profile of v1, /device:TPU:1, one launch (start us, length us, event | category | flops | bytes accessed | tf_op | source)
XLA Modules:
  0.0 258.5 jit_solution(3997585238691831217)
XLA Ops:
  0.0 1.8 stack.2
  1.8 8.3 %all-to-all-start = ((bf16[8,4,2,2048]{3,2,1,0:T(2,128)(2,1)}), bf16[8,4,2,2048]{3,2,1,0:T(2,128)(2,1)S(1)}, u32[]{:S(2)}, u32[]{:S(2)}) async-start(bf16[8,4,2,2048]{3,2,1,0:T(2,128)(2,1)} %stack.2), calls=%async_computation | async-start | bytes 524288 | tf_op jit(solution)/shard_map/all_to_all | solution.py:43
  10.1 0.8 reshape.74
  11.2 10.8 %gather_fusion = bf16[1024,4,512]{2,1,0:T(4,128)(2,1)} fusion(bf16[512,4,512]{2,1,0:T(4,128)(2,1)S(1)} %copy-done, s32[1024]{0:T(1024)S(1)} %fusion.16), kind=kCustom, calls=%fused_computation | custom fusion | bytes 8392704 | tf_op jit(solution)/shard_map/gather | solution.py:57
  22.0 6.5 %copy.95 = bf16[8,128,4,512]{3,2,0,1:T(4,128)(2,1)} copy(bf16[8,128,4,512]{3,2,1,0:T(4,128)(2,1)} %bitcast.55) | data formatting | bytes 8388608 | tf_op jit(solution)/shard_map/gather | solution.py:57
  28.5 10.8 %all-to-all-start.1 = ((bf16[8,128,4,512]{3,2,0,1:T(4,128)(2,1)}), bf16[8,128,4,512]{3,2,0,1:T(4,128)(2,1)}, u32[]{:S(2)}, u32[]{:S(2)}) async-start(bf16[8,128,4,512]{3,2,0,1:T(4,128)(2,1)} %copy.95), calls=%async_computation.1 | async-start | bytes 8388608 | tf_op jit(solution)/shard_map/all_to_all | solution.py:58
  39.7 60.0 %all_gather.6 = bf16[512,192]{1,0:T(8,128)(2,1)S(1)} all-gather(bf16[32,192]{1,0:T(8,128)(2,1)S(1)} %pad_maximum_fusion.1), channel_id=1, replica_groups=mesh['kt'=8,'ks'=16] {'ks'}, dimensions={0}, use_global_device_ids=true | all-gather | bytes 208896 | tf_op jit(solution)/shard_map/all_gather | solution.py:10
  100.1 30.6 %all_gather.7 = bf16[4,96,512]{1,0,2:T(4,128)(2,1)S(1)} all-gather(bf16[4,96,64]{1,0,2:T(4,128)(2,1)S(1)} %pad_maximum_fusion), channel_id=1, replica_groups=mesh['kt'=8,'ks'=16] {'kt'}, dimensions={2}, use_global_device_ids=true | all-gather | bytes 442368 | tf_op jit(solution)/shard_map/all_gather | solution.py:24
  130.7 0.4 split.8
  131.1 0.3 copy.113
  131.5 0.3 copy.111
  131.9 0.2 copy.90
  132.1 0.4 reshape_reshape.3
  132.5 0.7 convert_bitcast_fusion
  133.2 12.2 %copy.103 = bf16[4,16,32,512,1]{2,1,0,4,3:T(8,128)(2,1)} copy(bf16[4,16,32,512,1]{3,2,1,0,4:T(8,128)(2,1)S(1)} %convert_bitcast_fusion) | data formatting | bytes 4194304 | tf_op jit(solution)/shard_map/convert_element_type | solution.py:63
  145.3 5.6 %copy.96 = bf16[8,128,4,512]{3,2,1,0:T(4,128)(2,1)} copy(bf16[8,128,4,512]{3,2,0,1:T(4,128)(2,1)} %all-to-all-done.1) | data formatting | bytes 8388608 | tf_op jit(solution)/shard_map/all_to_all | solution.py:58
  150.9 6.9 %reshape.88 = bf16[2,4,512,512,1]{3,2,1,0,4:T(8,128)(2,1)} reshape(bf16[8,128,4,512]{3,2,1,0:T(4,128)(2,1)} %copy.96) | data formatting | bytes 8388608 | tf_op jit(solution)/shard_map/reshape | solution.py:59
  157.8 8.9 %fusion.3 = bf16[2,4,32,32,512]{4,3,2,1,0:T(8,128)(2,1)} fusion(f32[4,32,512]{2,1,0:T(8,128)S(1)} %convert_element_type.54, f32[2,32,512]{2,1,0:T(8,128)S(1)} %convert_bitcast_fusion.1, bf16[2,4,512,512,1]{3,2,1,0,4:T(8,128)(2,1)} %reshape.88), kind=kOutput, calls=%fused_computation.6 | convolution fusion | flops 4307550208 | bytes 12976128 | tf_op jit(solution)/shard_map/tsvwp,tspq->tsvwq/dot_general | solution.py:68
  166.8 44.3 %copy.98 = bf16[2,4,32,32,512]{3,2,1,0,4:T(8,128)(2,1)} copy(bf16[2,4,32,32,512]{4,3,2,1,0:T(8,128)(2,1)} %fusion.3) | data formatting | bytes 16777216 | tf_op jit(solution)/shard_map/convert_element_type | solution.py:70
  211.1 28.3 %fusion.4 = bf16[2,32,16,512]{1,2,0,3:T(8,128)(2,1)} fusion(bf16[4,16,32,512,1]{2,1,0,4,3:T(8,128)(2,1)} %copy.103, bf16[2,4,32,32,512]{3,2,1,0,4:T(8,128)(2,1)} %copy.98), kind=kOutput, calls=%fused_computation.7 | convolution fusion | flops 134742016 | bytes 11534336 | tf_op jit(solution)/shard_map/tsvwq,snwq->tvnq/dot_general | solution.py:71
  239.4 3.7 %fusion.11 = bf16[2,16,32,64]{3,2,1,0:T(8,128)(2,1)S(1)} fusion(bf16[2,64,512,1]{2,1,3,0:T(8,128)(2,1)S(1)} %bitcast.58, bf16[2,32,16,512]{1,2,0,3:T(8,128)(2,1)} %fusion.4), kind=kOutput, calls=%fused_computation.13 | convolution fusion | flops 67174400 | bytes 1310720 | tf_op jit(solution)/shard_map/tvnq,tcq->tnvc/dot_general | solution.py:74
  243.1 0.3 convert_element_type.61
  243.5 14.2 %all_to_all.15 = bf16[16,2,1,2048]{3,1,2,0:T(2,128)(2,1)S(1)} all-to-all(bf16[16,2,1,2048]{3,1,2,0:T(2,128)(2,1)S(1)} %bitcast.60), channel_id=1, replica_groups=mesh['kt'=8,'ks'=16] {'ks'}, dimensions={0} | all-to-all | bytes 262144 | tf_op jit(solution)/shard_map/all_to_all | solution.py:34
  257.8 0.6 reduce_sum.12
  (32 shorter events, 1.5 us)
Async XLA Ops:
  0.0 11.2 %copy-start = (bf16[512,4,512]{2,1,0:T(4,128)(2,1)S(1)}, bf16[512,4,512]{2,1,0:T(4,128)(2,1)}, u32[]{:S(2)}) copy-start(bf16[512,4,512]{2,1,0:T(4,128)(2,1)} %param.12) | copy-start | bytes 6291460
  1.8 26.7 %all-to-all-start = ((bf16[8,4,2,2048]{3,2,1,0:T(2,128)(2,1)}), bf16[8,4,2,2048]{3,2,1,0:T(2,128)(2,1)S(1)}, u32[]{:S(2)}, u32[]{:S(2)}) async-start(bf16[8,4,2,2048]{3,2,1,0:T(2,128)(2,1)} %stack.2), calls=%async_computation | async-start | bytes 524288 | tf_op jit(solution)/shard_map/all_to_all | solution.py:43
  28.5 10.9 %copy-start.5 = (bf16[2,64,32]{1,2,0:T(8,128)(2,1)S(1)}, bf16[2,64,32]{1,2,0:T(8,128)(2,1)}, u32[]{:S(2)}) copy-start(bf16[2,64,32]{1,2,0:T(8,128)(2,1)} %param.8) | copy-start | bytes 24580
  28.5 11.0 %copy-start.4 = (bf16[2,32,32]{2,1,0:T(8,128)(2,1)S(1)}, bf16[2,32,32]{2,1,0:T(8,128)(2,1)}, u32[]{:S(2)}) copy-start(bf16[2,32,32]{2,1,0:T(8,128)(2,1)} %param.7) | copy-start | bytes 12292
  28.5 71.2 %copy-start.3 = (bf16[4,32,64]{2,1,0:T(8,128)(2,1)S(1)}, bf16[4,32,64]{2,1,0:T(8,128)(2,1)}, u32[]{:S(2)}) copy-start(bf16[4,32,64]{2,1,0:T(8,128)(2,1)} %param.9) | copy-start | bytes 49156
  28.5 71.4 %copy-start.2 = (bf16[4,64,64]{2,1,0:T(8,128)(2,1)S(1)}, bf16[4,64,64]{2,1,0:T(8,128)(2,1)}, u32[]{:S(2)}) copy-start(bf16[4,64,64]{2,1,0:T(8,128)(2,1)} %param.10) | copy-start | bytes 98308
  28.5 116.8 %all-to-all-start.1 = ((bf16[8,128,4,512]{3,2,0,1:T(4,128)(2,1)}), bf16[8,128,4,512]{3,2,0,1:T(4,128)(2,1)}, u32[]{:S(2)}, u32[]{:S(2)}) async-start(bf16[8,128,4,512]{3,2,0,1:T(4,128)(2,1)} %copy.95), calls=%async_computation.1 | async-start | bytes 8388608 | tf_op jit(solution)/shard_map/all_to_all | solution.py:58
  211.1 47.4 %copy-start.1 = (bf16[512,4,512]{2,1,0:T(4,128)(2,1)S(1)}, bf16[512,4,512]{2,1,0:T(4,128)(2,1)}, u32[]{:S(2)}) copy-start(bf16[512,4,512]{2,1,0:T(4,128)(2,1)} %param.12) | copy-start | bytes 6291460
